TPU v7x, 128 devices: a whole 4x4x4 slice. The times are simulated.
128 devices in a mesh: section: 8 (over y, core), edge: 16 (over z, x).
Axes of the slice: x: 4, y: 4, z: 4, core: 2. Of those that a mesh axis runs over, the one named last changes fastest.
Arguments:
- layer_nodes: bfloat16 [8, 2, 256, 512], P('section'), may hold values from -6 to 6
- layer_edges: bfloat16 [8, 2, 4096, 512], P('section', None, 'edge'), may hold values from -6 to 6
- top_nodes: bfloat16 [2, 256, 512], replicated, may hold values from -1.5 to 1.5
- top_edges: bfloat16 [2, 4096, 512], P(None, 'edge'), may hold values from -1.5 to 1.5
- tile_blocks: int32 [2, 32, 2], P(None, 'edge'), may hold values from 0 to 1
- senders: int32 [2, 4096], P(None, 'edge'), may hold values from 0 to 127
- receivers: int32 [2, 4096], P(None, 'edge'), may hold values from 0 to 127
- w_send: bfloat16 [8, 512, 512], P('section'), may hold values from -0.0625 to 0.0625
- w_recv: bfloat16 [8, 512, 512], P('section'), may hold values from -0.0625 to 0.0625
- w_edge: bfloat16 [8, 512, 512], P('section'), may hold values from -0.25 to 0.25
- w_msg: bfloat16 [8, 512, 512], P('section'), may hold values from -0.125 to 0.125
- w_node: bfloat16 [8, 512, 512], P('section'), may hold values from -0.25 to 0.25
- w_agg: bfloat16 [8, 512, 512], P('section'), may hold values from -0.25 to 0.25
- w_out: bfloat16 [8, 512, 512], P('section'), may hold values from -0.125 to 0.125
Outputs:
- node_grads: bfloat16 [8, 2, 256, 512], P('section', None, 'edge')
- edge_grads: bfloat16 [8, 2, 4096, 512], P('section', None, 'edge')
- g_send: float32 [8, 512, 512], P('section', 'edge')
- g_recv: float32 [8, 512, 512], P('section', 'edge')
- g_edge: float32 [8, 512, 512], P('section', 'edge')
- g_msg: float32 [8, 512, 512], P('section', 'edge')
- g_node: float32 [8, 512, 512], P('section', 'edge')
- g_agg: float32 [8, 512, 512], P('section', 'edge')
- g_out: float32 [8, 512, 512], P('section', 'edge')
All inputs are finite; a program needn't handle non-finite values.
Results may differ from a plain program's by a relative error of at most 0.029.
Values may be sent and summed in bfloat16 or wider, within the bound.
A program may use at most 64 MiB of HBM per device.

v0:
```python
import jax
import jax.numpy as jnp
from jax import lax
from jax.sharding import PartitionSpec as P

BLOCK = 128


def shifted(shard, axis, by):
    peers = lax.axis_size(axis)
    pairs = [(i, i + by) for i in range(peers) if 0 <= i + by < peers]
    return lax.ppermute(shard, axis, pairs)


def silu_slope(values):
    sigma = jax.nn.sigmoid(values)
    return sigma * (1.0 + values * (1.0 - sigma))


def matmul(left, right):
    return jnp.dot(left, right, preferred_element_type=jnp.float32)


def times_transposed(left, right):
    return lax.dot_general(
        left, right, (((1,), (1,)), ((), ())), preferred_element_type=jnp.float32
    )


def transposed_times(left, right):
    return lax.dot_general(
        left, right, (((0,), (0,)), ((), ())), preferred_element_type=jnp.float32
    )


def to_edges(values, block_hot, edge_hot):
    width = values.shape[1]
    grouped = values.reshape(block_hot.shape[1], -1, width)
    picked = jnp.einsum(
        "tb,bcd->tcd", block_hot, grouped, preferred_element_type=jnp.float32
    ).astype(jnp.bfloat16)
    spread = jnp.einsum("tec,tcd->ted", edge_hot, picked, preferred_element_type=jnp.float32)
    return spread.reshape(-1, width).astype(jnp.bfloat16)


def to_nodes(values, block_hot, edge_hot):
    width = values.shape[1]
    per_tile = jnp.einsum(
        "tec,ted->tcd",
        edge_hot,
        values.reshape(block_hot.shape[0], -1, width),
        preferred_element_type=jnp.float32,
    )
    summed = jnp.einsum(
        "tb,tcd->bcd", block_hot.astype(jnp.float32), per_tile, precision=lax.Precision.HIGHEST
    )
    return summed.reshape(-1, width)


def body(
    layer_nodes,
    layer_edges,
    top_nodes,
    top_edges,
    tile_blocks,
    senders,
    receivers,
    w_send,
    w_recv,
    w_edge,
    w_msg,
    w_node,
    w_agg,
    w_out,
):
    sections = lax.axis_size("section")
    section = lax.axis_index("section")
    groups = lax.axis_size("edge")
    member = lax.axis_index("edge")
    nodes_all = layer_nodes[0]
    edges_all = layer_edges[0]
    batches = nodes_all.shape[0]
    node_count = nodes_all.shape[1]
    width = nodes_all.shape[2]
    tile_count = tile_blocks.shape[1]
    tile_len = edges_all.shape[1] // tile_count
    block_count = node_count // BLOCK
    row_count = node_count // groups
    weight_send, weight_recv, weight_edge, weight_msg = (w_send[0], w_recv[0], w_edge[0], w_msg[0])
    weight_node, weight_agg, weight_out = (w_node[0], w_agg[0], w_out[0])
    lanes = jnp.arange(BLOCK, dtype=jnp.int32)
    slots = jnp.arange(block_count, dtype=jnp.int32)
    send_hot = (senders.reshape(batches, tile_count, tile_len)[..., None] == lanes).astype(
        jnp.bfloat16
    )
    recv_hot = (receivers.reshape(batches, tile_count, tile_len)[..., None] == lanes).astype(
        jnp.bfloat16
    )
    send_block = (tile_blocks[:, :, 0][..., None] == slots).astype(jnp.bfloat16)
    recv_block = (tile_blocks[:, :, 1][..., None] == slots).astype(jnp.bfloat16)

    def advance(moment, carry):
        node_in_grad, edge_in_grad, totals, node_record, edge_record = carry
        batch_raw = moment - (sections - 1 - section)
        valid = (batch_raw >= 0) & (batch_raw < batches)
        batch = jnp.clip(batch_raw, 0, batches - 1)
        feats = lax.dynamic_index_in_dim(nodes_all, batch, 0, keepdims=False)
        edge_feats = lax.dynamic_index_in_dim(edges_all, batch, 0, keepdims=False)
        send_tiles = lax.dynamic_index_in_dim(send_hot, batch, 0, keepdims=False)
        recv_tiles = lax.dynamic_index_in_dim(recv_hot, batch, 0, keepdims=False)
        send_blocks = lax.dynamic_index_in_dim(send_block, batch, 0, keepdims=False)
        recv_blocks = lax.dynamic_index_in_dim(recv_block, batch, 0, keepdims=False)
        top_node = lax.dynamic_index_in_dim(top_nodes, batch, 0, keepdims=False)
        top_edge = lax.dynamic_index_in_dim(top_edges, batch, 0, keepdims=False)
        is_last = section == sections - 1
        grad_nodes = jnp.where(is_last, top_node, node_in_grad)
        grad_edges = jnp.where(is_last, top_edge, edge_in_grad)
        send_feats = to_edges(feats, send_blocks, send_tiles)
        recv_feats = to_edges(feats, recv_blocks, recv_tiles)
        pre = (
            matmul(send_feats, weight_send)
            + matmul(recv_feats, weight_recv)
            + matmul(edge_feats, weight_edge)
        )
        act = jax.nn.silu(pre).astype(jnp.bfloat16)
        message = matmul(act, weight_msg).astype(jnp.bfloat16)
        partial_agg = to_nodes(message, recv_blocks, recv_tiles)
        aggregate = lax.psum(partial_agg, "edge")
        agg_b = aggregate.astype(jnp.bfloat16)
        node_pre = matmul(feats, weight_node) + matmul(agg_b, weight_agg)
        node_act = jax.nn.silu(node_pre).astype(jnp.bfloat16)
        node_delta = (times_transposed(grad_nodes, weight_out) * silu_slope(node_pre)).astype(
            jnp.bfloat16
        )
        agg_grad = times_transposed(node_delta, weight_agg).astype(jnp.bfloat16)
        node_term = times_transposed(node_delta, weight_node)
        agg_edges = to_edges(agg_grad, recv_blocks, recv_tiles)
        message_grad = (grad_edges.astype(jnp.float32) + agg_edges.astype(jnp.float32)).astype(
            jnp.bfloat16
        )
        edge_delta = (times_transposed(message_grad, weight_msg) * silu_slope(pre)).astype(
            jnp.bfloat16
        )
        edge_out = (
            grad_edges.astype(jnp.float32) + times_transposed(edge_delta, weight_edge)
        ).astype(jnp.bfloat16)
        send_grad = times_transposed(edge_delta, weight_send).astype(jnp.bfloat16)
        recv_grad = times_transposed(edge_delta, weight_recv).astype(jnp.bfloat16)
        partial_back = to_nodes(send_grad, send_blocks, send_tiles) + to_nodes(
            recv_grad, recv_blocks, recv_tiles
        )
        edge_terms = lax.psum(partial_back, "edge")
        node_out = (grad_nodes.astype(jnp.float32) + node_term + edge_terms).astype(jnp.bfloat16)
        fresh = (
            transposed_times(send_feats, edge_delta),
            transposed_times(recv_feats, edge_delta),
            transposed_times(edge_feats, edge_delta),
            transposed_times(act, message_grad),
            transposed_times(feats, node_delta),
            transposed_times(agg_b, node_delta),
            transposed_times(node_act, grad_nodes),
        )
        totals = tuple(
            (jnp.where(valid, before + extra, before) for before, extra in zip(totals, fresh))
        )
        own_out = lax.dynamic_slice_in_dim(node_out, member * row_count, row_count, 0)
        node_record = jnp.where(
            valid, lax.dynamic_update_index_in_dim(node_record, own_out, batch, 0), node_record
        )
        edge_record = jnp.where(
            valid, lax.dynamic_update_index_in_dim(edge_record, edge_out, batch, 0), edge_record
        )
        sent_nodes, sent_edges = shifted((node_out, edge_out), "section", -1)
        return (sent_nodes, sent_edges, totals, node_record, edge_record)

    hidden = weight_send.shape[1]
    square_in = jnp.zeros((width, hidden), jnp.float32)
    square_back = jnp.zeros((hidden, width), jnp.float32)
    start = (
        jnp.zeros((node_count, width), jnp.bfloat16),
        jnp.zeros(edges_all.shape[1:], jnp.bfloat16),
        (square_in, square_in, square_in, square_back, square_in, square_in, square_back),
        jnp.zeros((batches, row_count, width), jnp.bfloat16),
        jnp.zeros(edges_all.shape, jnp.bfloat16),
    )
    finished = lax.fori_loop(0, sections + batches - 1, advance, start)
    totals, node_record, edge_record = (finished[2], finished[3], finished[4])
    sum_send, sum_recv, sum_edge, sum_msg, sum_node, sum_agg, sum_out = totals
    sum_send, sum_recv, sum_edge, sum_msg = (
        lax.psum_scatter(sum_send, "edge", scatter_dimension=0, tiled=True),
        lax.psum_scatter(sum_recv, "edge", scatter_dimension=0, tiled=True),
        lax.psum_scatter(sum_edge, "edge", scatter_dimension=0, tiled=True),
        lax.psum_scatter(sum_msg, "edge", scatter_dimension=0, tiled=True),
    )
    sum_node = lax.dynamic_slice_in_dim(sum_node, member * (width // groups), width // groups, 0)
    sum_agg = lax.dynamic_slice_in_dim(sum_agg, member * (width // groups), width // groups, 0)
    sum_out = lax.dynamic_slice_in_dim(sum_out, member * (hidden // groups), hidden // groups, 0)
    return (
        node_record[None],
        edge_record[None],
        sum_send[None],
        sum_recv[None],
        sum_edge[None],
        sum_msg[None],
        sum_node[None],
        sum_agg[None],
        sum_out[None],
    )


def solution(mesh):
    in_specs = (
        P("section", None, None, None),
        P("section", None, "edge", None),
        P(),
        P(None, "edge", None),
        P(None, "edge", None),
        P(None, "edge"),
        P(None, "edge"),
        P("section", None, None),
        P("section", None, None),
        P("section", None, None),
        P("section", None, None),
        P("section", None, None),
        P("section", None, None),
        P("section", None, None),
    )
    out_specs = (
        P("section", None, "edge", None),
        P("section", None, "edge", None),
        P("section", "edge", None),
        P("section", "edge", None),
        P("section", "edge", None),
        P("section", "edge", None),
        P("section", "edge", None),
        P("section", "edge", None),
        P("section", "edge", None),
    )
    return jax.shard_map(body, mesh=mesh, in_specs=in_specs, out_specs=out_specs, check_vma=False)
```

profile of v0, /device:TPU:0, one launch (start us, length us, event | category | flops | bytes accessed | tf_op | source)
XLA Modules:
  0.0 2031.3 jit_solution(16253940211328947030)
XLA Ops:
  13.3 1701.8 %while.36 = (s32[]{:T(128)}, bf16[256,512]{1,0:T(8,128)(2,1)S(1)}, bf16[256,512]{1,0:T(8,128)(2,1)S(1)}, f32[512,512]{1,0:T(8,128)}, f32[512,512]{1,0:T(8,128)},...) while((s32[]{:T(128)}, bf16[256,512]{1,0:T(8,128)(2,1)S(1)}, ...), condition=%wide.region_3.4_spmd.clone, body=%wide.region_0.3_spmd.clone.sunk | while | flops 2910199808 | bytes 137546704 | solution.py:186
  21.1 81.4 %all-reduce.4 = bf16[256,512]{1,0:T(8,128)(2,1)S(1)} all-reduce(f32[256,512]{1,0:T(8,128)S(1)} %bitcast.271), channel_id=1, replica_groups=mesh['section'=8,'edge'=16] {'edge'}, use_global_device_ids=true, to_apply=%region_1.1 | all-reduce | flops 131072 | bytes 786432 | tf_op jit(solution)/shard_map/while/body/eval_jaxpr/psum | solution.py:128
  129.5 69.2 %all-reduce.3.cloned.1.call-done = f32[256,512]{1,0:T(8,128)} async-done(((f32[256,512]{1,0:T(8,128)}), f32[256,512]{1,0:T(8,128)}) %all-reduce.3.cloned.1.call-update) | async-done | bytes 524304 | tf_op jit(solution)/shard_map/while/body/eval_jaxpr/psum | solution.py:152
  211.4 77.6 %all-reduce.4 = bf16[256,512]{1,0:T(8,128)(2,1)S(1)} all-reduce(f32[256,512]{1,0:T(8,128)S(1)} %bitcast.271), channel_id=1, replica_groups=mesh['section'=8,'edge'=16] {'edge'}, use_global_device_ids=true, to_apply=%region_1.1 | all-reduce | flops 131072 | bytes 786432 | tf_op jit(solution)/shard_map/while/body/eval_jaxpr/psum | solution.py:128
  317.5 70.1 %all-reduce.3.cloned.1.call-done = f32[256,512]{1,0:T(8,128)} async-done(((f32[256,512]{1,0:T(8,128)}), f32[256,512]{1,0:T(8,128)}) %all-reduce.3.cloned.1.call-update) | async-done | bytes 524304 | tf_op jit(solution)/shard_map/while/body/eval_jaxpr/psum | solution.py:152
  400.3 77.6 %all-reduce.4 = bf16[256,512]{1,0:T(8,128)(2,1)S(1)} all-reduce(f32[256,512]{1,0:T(8,128)S(1)} %bitcast.271), channel_id=1, replica_groups=mesh['section'=8,'edge'=16] {'edge'}, use_global_device_ids=true, to_apply=%region_1.1 | all-reduce | flops 131072 | bytes 786432 | tf_op jit(solution)/shard_map/while/body/eval_jaxpr/psum | solution.py:128
  506.5 70.1 %all-reduce.3.cloned.1.call-done = f32[256,512]{1,0:T(8,128)} async-done(((f32[256,512]{1,0:T(8,128)}), f32[256,512]{1,0:T(8,128)}) %all-reduce.3.cloned.1.call-update) | async-done | bytes 524304 | tf_op jit(solution)/shard_map/while/body/eval_jaxpr/psum | solution.py:152
  589.3 77.6 %all-reduce.4 = bf16[256,512]{1,0:T(8,128)(2,1)S(1)} all-reduce(f32[256,512]{1,0:T(8,128)S(1)} %bitcast.271), channel_id=1, replica_groups=mesh['section'=8,'edge'=16] {'edge'}, use_global_device_ids=true, to_apply=%region_1.1 | all-reduce | flops 131072 | bytes 786432 | tf_op jit(solution)/shard_map/while/body/eval_jaxpr/psum | solution.py:128
  695.4 70.1 %all-reduce.3.cloned.1.call-done = f32[256,512]{1,0:T(8,128)} async-done(((f32[256,512]{1,0:T(8,128)}), f32[256,512]{1,0:T(8,128)}) %all-reduce.3.cloned.1.call-update) | async-done | bytes 524304 | tf_op jit(solution)/shard_map/while/body/eval_jaxpr/psum | solution.py:152
  778.2 77.6 %all-reduce.4 = bf16[256,512]{1,0:T(8,128)(2,1)S(1)} all-reduce(f32[256,512]{1,0:T(8,128)S(1)} %bitcast.271), channel_id=1, replica_groups=mesh['section'=8,'edge'=16] {'edge'}, use_global_device_ids=true, to_apply=%region_1.1 | all-reduce | flops 131072 | bytes 786432 | tf_op jit(solution)/shard_map/while/body/eval_jaxpr/psum | solution.py:128
  884.4 70.1 %all-reduce.3.cloned.1.call-done = f32[256,512]{1,0:T(8,128)} async-done(((f32[256,512]{1,0:T(8,128)}), f32[256,512]{1,0:T(8,128)}) %all-reduce.3.cloned.1.call-update) | async-done | bytes 524304 | tf_op jit(solution)/shard_map/while/body/eval_jaxpr/psum | solution.py:152
  967.2 77.6 %all-reduce.4 = bf16[256,512]{1,0:T(8,128)(2,1)S(1)} all-reduce(f32[256,512]{1,0:T(8,128)S(1)} %bitcast.271), channel_id=1, replica_groups=mesh['section'=8,'edge'=16] {'edge'}, use_global_device_ids=true, to_apply=%region_1.1 | all-reduce | flops 131072 | bytes 786432 | tf_op jit(solution)/shard_map/while/body/eval_jaxpr/psum | solution.py:128
  1073.3 70.1 %all-reduce.3.cloned.1.call-done = f32[256,512]{1,0:T(8,128)} async-done(((f32[256,512]{1,0:T(8,128)}), f32[256,512]{1,0:T(8,128)}) %all-reduce.3.cloned.1.call-update) | async-done | bytes 524304 | tf_op jit(solution)/shard_map/while/body/eval_jaxpr/psum | solution.py:152
  1156.1 77.6 %all-reduce.4 = bf16[256,512]{1,0:T(8,128)(2,1)S(1)} all-reduce(f32[256,512]{1,0:T(8,128)S(1)} %bitcast.271), channel_id=1, replica_groups=mesh['section'=8,'edge'=16] {'edge'}, use_global_device_ids=true, to_apply=%region_1.1 | all-reduce | flops 131072 | bytes 786432 | tf_op jit(solution)/shard_map/while/body/eval_jaxpr/psum | solution.py:128
  1262.3 70.1 %all-reduce.3.cloned.1.call-done = f32[256,512]{1,0:T(8,128)} async-done(((f32[256,512]{1,0:T(8,128)}), f32[256,512]{1,0:T(8,128)}) %all-reduce.3.cloned.1.call-update) | async-done | bytes 524304 | tf_op jit(solution)/shard_map/while/body/eval_jaxpr/psum | solution.py:152
  1345.1 77.6 %all-reduce.4 = bf16[256,512]{1,0:T(8,128)(2,1)S(1)} all-reduce(f32[256,512]{1,0:T(8,128)S(1)} %bitcast.271), channel_id=1, replica_groups=mesh['section'=8,'edge'=16] {'edge'}, use_global_device_ids=true, to_apply=%region_1.1 | all-reduce | flops 131072 | bytes 786432 | tf_op jit(solution)/shard_map/while/body/eval_jaxpr/psum | solution.py:128
  1440.4 2.9 add_select_fusion.17
  1451.2 70.1 %all-reduce.3.cloned.1.call-done = f32[256,512]{1,0:T(8,128)} async-done(((f32[256,512]{1,0:T(8,128)}), f32[256,512]{1,0:T(8,128)}) %all-reduce.3.cloned.1.call-update) | async-done | bytes 524304 | tf_op jit(solution)/shard_map/while/body/eval_jaxpr/psum | solution.py:152
  1534.1 77.6 %all-reduce.4 = bf16[256,512]{1,0:T(8,128)(2,1)S(1)} all-reduce(f32[256,512]{1,0:T(8,128)S(1)} %bitcast.271), channel_id=1, replica_groups=mesh['section'=8,'edge'=16] {'edge'}, use_global_device_ids=true, to_apply=%region_1.1 | all-reduce | flops 131072 | bytes 786432 | tf_op jit(solution)/shard_map/while/body/eval_jaxpr/psum | solution.py:128
  1640.2 70.1 %all-reduce.3.cloned.1.call-done = f32[256,512]{1,0:T(8,128)} async-done(((f32[256,512]{1,0:T(8,128)}), f32[256,512]{1,0:T(8,128)}) %all-reduce.3.cloned.1.call-update) | async-done | bytes 524304 | tf_op jit(solution)/shard_map/while/body/eval_jaxpr/psum | solution.py:152
  1722.0 73.1 %reduce-scatter.5.cloned.1.call-done = f32[32,512]{1,0:T(8,128)} async-done(((f32[512,512]{1,0:T(8,128)}), f32[32,512]{1,0:T(8,128)}) %reduce-scatter.5.cloned.1.call-update) | async-done | bytes 65552 | tf_op jit(solution)/shard_map/reduce_scatter | solution.py:190
  1795.1 76.3 %reduce-scatter.7.cloned.1.call-done = f32[32,512]{1,0:T(8,128)} async-done(((f32[512,512]{1,0:T(8,128)}), f32[32,512]{1,0:T(8,128)}) %reduce-scatter.7.cloned.1.call-update) | async-done | bytes 65552 | tf_op jit(solution)/shard_map/reduce_scatter | solution.py:191
  1871.4 76.0 %reduce-scatter.9.cloned.1.call-done = f32[32,512]{1,0:T(8,128)} async-done(((f32[512,512]{1,0:T(8,128)}), f32[32,512]{1,0:T(8,128)}) %reduce-scatter.9.cloned.1.call-update) | async-done | bytes 65552 | tf_op jit(solution)/shard_map/reduce_scatter | solution.py:192
  1947.4 76.5 %reduce-scatter.11.cloned.1.call-done = f32[32,512]{1,0:T(8,128)} async-done(((f32[512,512]{1,0:T(8,128)}), f32[32,512]{1,0:T(8,128)}) %reduce-scatter.11.cloned.1.call-update) | async-done | bytes 65552 | tf_op jit(solution)/shard_map/reduce_scatter | solution.py:193
  (999 shorter events, 374.4 us)
Async XLA Ops:
  13.3 185.4 %all-reduce.3.cloned.1.call-start = ((), (), s32[]{:S(2)}) async-start(), calls=%async_computation.8 | async-start | bytes 1048576 | tf_op jit(solution)/shard_map/while/body/eval_jaxpr/psum | solution.py:152
  119.0 83.2 %collective-permute-start.1 = (bf16[256,512]{1,0:T(8,128)(2,1)}, bf16[256,512]{1,0:T(8,128)(2,1)S(1)}, u32[]{:S(2)}, u32[]{:S(2)}) collective-permute-start(bf16[256,512]{1,0:T(8,128)(2,1)} %get-tuple-element.1012), channel_id=1, source_target_pairs={{16,0},{32,16},{48,32},{64,48},{80,64},{96,80},{112,96},{17,1},{33... | collective-permute-start | bytes 786440 | tf_op jit(solution)/shard_map/while/body/eval_jaxpr/ppermute | solution.py:12
  203.5 184.1 %all-reduce.3.cloned.1.call-start = ((), (), s32[]{:S(2)}) async-start(), calls=%async_computation.8 | async-start | bytes 1048576 | tf_op jit(solution)/shard_map/while/body/eval_jaxpr/psum | solution.py:152
  305.4 85.7 %collective-permute-start.1 = (bf16[256,512]{1,0:T(8,128)(2,1)}, bf16[256,512]{1,0:T(8,128)(2,1)S(1)}, u32[]{:S(2)}, u32[]{:S(2)}) collective-permute-start(bf16[256,512]{1,0:T(8,128)(2,1)} %get-tuple-element.1012), channel_id=1, source_target_pairs={{16,0},{32,16},{48,32},{64,48},{80,64},{96,80},{112,96},{17,1},{33... | collective-permute-start | bytes 786440 | tf_op jit(solution)/shard_map/while/body/eval_jaxpr/ppermute | solution.py:12
  392.5 184.1 %all-reduce.3.cloned.1.call-start = ((), (), s32[]{:S(2)}) async-start(), calls=%async_computation.8 | async-start | bytes 1048576 | tf_op jit(solution)/shard_map/while/body/eval_jaxpr/psum | solution.py:152
  494.4 85.7 %collective-permute-start.1 = (bf16[256,512]{1,0:T(8,128)(2,1)}, bf16[256,512]{1,0:T(8,128)(2,1)S(1)}, u32[]{:S(2)}, u32[]{:S(2)}) collective-permute-start(bf16[256,512]{1,0:T(8,128)(2,1)} %get-tuple-element.1012), channel_id=1, source_target_pairs={{16,0},{32,16},{48,32},{64,48},{80,64},{96,80},{112,96},{17,1},{33... | collective-permute-start | bytes 786440 | tf_op jit(solution)/shard_map/while/body/eval_jaxpr/ppermute | solution.py:12
  578.0 3.4 collective-permute-start
  581.4 184.1 %all-reduce.3.cloned.1.call-start = ((), (), s32[]{:S(2)}) async-start(), calls=%async_computation.8 | async-start | bytes 1048576 | tf_op jit(solution)/shard_map/while/body/eval_jaxpr/psum | solution.py:152
  683.3 85.7 %collective-permute-start.1 = (bf16[256,512]{1,0:T(8,128)(2,1)}, bf16[256,512]{1,0:T(8,128)(2,1)S(1)}, u32[]{:S(2)}, u32[]{:S(2)}) collective-permute-start(bf16[256,512]{1,0:T(8,128)(2,1)} %get-tuple-element.1012), channel_id=1, source_target_pairs={{16,0},{32,16},{48,32},{64,48},{80,64},{96,80},{112,96},{17,1},{33... | collective-permute-start | bytes 786440 | tf_op jit(solution)/shard_map/while/body/eval_jaxpr/ppermute | solution.py:12
  766.9 3.4 collective-permute-start
  770.4 184.1 %all-reduce.3.cloned.1.call-start = ((), (), s32[]{:S(2)}) async-start(), calls=%async_computation.8 | async-start | bytes 1048576 | tf_op jit(solution)/shard_map/while/body/eval_jaxpr/psum | solution.py:152
  872.3 85.7 %collective-permute-start.1 = (bf16[256,512]{1,0:T(8,128)(2,1)}, bf16[256,512]{1,0:T(8,128)(2,1)S(1)}, u32[]{:S(2)}, u32[]{:S(2)}) collective-permute-start(bf16[256,512]{1,0:T(8,128)(2,1)} %get-tuple-element.1012), channel_id=1, source_target_pairs={{16,0},{32,16},{48,32},{64,48},{80,64},{96,80},{112,96},{17,1},{33... | collective-permute-start | bytes 786440 | tf_op jit(solution)/shard_map/while/body/eval_jaxpr/ppermute | solution.py:12
  959.3 184.1 %all-reduce.3.cloned.1.call-start = ((), (), s32[]{:S(2)}) async-start(), calls=%async_computation.8 | async-start | bytes 1048576 | tf_op jit(solution)/shard_map/while/body/eval_jaxpr/psum | solution.py:152
  1061.2 85.7 %collective-permute-start.1 = (bf16[256,512]{1,0:T(8,128)(2,1)}, bf16[256,512]{1,0:T(8,128)(2,1)S(1)}, u32[]{:S(2)}, u32[]{:S(2)}) collective-permute-start(bf16[256,512]{1,0:T(8,128)(2,1)} %get-tuple-element.1012), channel_id=1, source_target_pairs={{16,0},{32,16},{48,32},{64,48},{80,64},{96,80},{112,96},{17,1},{33... | collective-permute-start | bytes 786440 | tf_op jit(solution)/shard_map/while/body/eval_jaxpr/ppermute | solution.py:12
  1148.3 184.1 %all-reduce.3.cloned.1.call-start = ((), (), s32[]{:S(2)}) async-start(), calls=%async_computation.8 | async-start | bytes 1048576 | tf_op jit(solution)/shard_map/while/body/eval_jaxpr/psum | solution.py:152
  1250.2 85.7 %collective-permute-start.1 = (bf16[256,512]{1,0:T(8,128)(2,1)}, bf16[256,512]{1,0:T(8,128)(2,1)S(1)}, u32[]{:S(2)}, u32[]{:S(2)}) collective-permute-start(bf16[256,512]{1,0:T(8,128)(2,1)} %get-tuple-element.1012), channel_id=1, source_target_pairs={{16,0},{32,16},{48,32},{64,48},{80,64},{96,80},{112,96},{17,1},{33... | collective-permute-start | bytes 786440 | tf_op jit(solution)/shard_map/while/body/eval_jaxpr/ppermute | solution.py:12
  1337.2 184.1 %all-reduce.3.cloned.1.call-start = ((), (), s32[]{:S(2)}) async-start(), calls=%async_computation.8 | async-start | bytes 1048576 | tf_op jit(solution)/shard_map/while/body/eval_jaxpr/psum | solution.py:152
  1439.1 85.7 %collective-permute-start.1 = (bf16[256,512]{1,0:T(8,128)(2,1)}, bf16[256,512]{1,0:T(8,128)(2,1)S(1)}, u32[]{:S(2)}, u32[]{:S(2)}) collective-permute-start(bf16[256,512]{1,0:T(8,128)(2,1)} %get-tuple-element.1012), channel_id=1, source_target_pairs={{16,0},{32,16},{48,32},{64,48},{80,64},{96,80},{112,96},{17,1},{33... | collective-permute-start | bytes 786440 | tf_op jit(solution)/shard_map/while/body/eval_jaxpr/ppermute | solution.py:12
  1526.2 184.1 %all-reduce.3.cloned.1.call-start = ((), (), s32[]{:S(2)}) async-start(), calls=%async_computation.8 | async-start | bytes 1048576 | tf_op jit(solution)/shard_map/while/body/eval_jaxpr/psum | solution.py:152
  1628.1 85.7 %collective-permute-start.1 = (bf16[256,512]{1,0:T(8,128)(2,1)}, bf16[256,512]{1,0:T(8,128)(2,1)S(1)}, u32[]{:S(2)}, u32[]{:S(2)}) collective-permute-start(bf16[256,512]{1,0:T(8,128)(2,1)} %get-tuple-element.1012), channel_id=1, source_target_pairs={{16,0},{32,16},{48,32},{64,48},{80,64},{96,80},{112,96},{17,1},{33... | collective-permute-start | bytes 786440 | tf_op jit(solution)/shard_map/while/body/eval_jaxpr/ppermute | solution.py:12
  1715.1 80.0 %reduce-scatter.5.cloned.1.call-start = ((), (), s32[]{:S(2)}) async-start(), calls=%async_computation.4 | async-start | bytes 1114112 | tf_op jit(solution)/shard_map/reduce_scatter | solution.py:190
  1715.7 155.7 %reduce-scatter.7.cloned.1.call-start = ((), (), s32[]{:S(2)}) async-start(), calls=%async_computation.5 | async-start | bytes 1114112 | tf_op jit(solution)/shard_map/reduce_scatter | solution.py:191
  1716.3 231.1 %reduce-scatter.9.cloned.1.call-start = ((), (), s32[]{:S(2)}) async-start(), calls=%async_computation.6 | async-start | bytes 1114112 | tf_op jit(solution)/shard_map/reduce_scatter | solution.py:192
  1716.9 307.1 %reduce-scatter.11.cloned.1.call-start = ((), (), s32[]{:S(2)}) async-start(), calls=%async_computation.7 | async-start | bytes 1114112 | tf_op jit(solution)/shard_map/reduce_scatter | solution.py:193
  (291 other events, 1022.0 us)
Sparse Core Ops, SparseCore 0:
  115.9 82.6 all-reduce.2
  302.4 85.1 all-reduce.2
  491.3 85.1 all-reduce.2
  680.3 85.1 all-reduce.2
  869.2 85.1 all-reduce.2
  1058.2 85.1 all-reduce.2
  1247.1 85.1 all-reduce.2
  1436.1 85.1 all-reduce.2
  1625.0 85.1 all-reduce.2
Sparse Core Ops, SparseCore 1:
  1719.4 75.7 reduce-scatter.4
  1799.1 72.2 reduce-scatter.6
  1875.0 72.3 reduce-scatter.8
  1951.5 72.4 reduce-scatter.10
where the time goes:
time: 2040 us; the launch traced here: 2030 us
  waiting for transfers between devices  946 us (46%)
  blocking collectives  702 us (34%)
  matrix products  214 us (10%)
  local copies, waits for them, and re-layouts  123 us (6%)
  starting transfers between devices  23.3 us (1%)
    psum x9, blocking collectives, advance(): aggregate = lax.psum(partial_agg, 'edge')  702 us
    psum x9, waiting for transfers between devices, advance(): edge_terms = lax.psum(partial_back, 'edge')  630 us
    while x558, local copies, waits for them, and re-layouts  96.3 us
    reduce_scatter x1, waiting for transfers between devices, body(): lax.psum_scatter(sum_msg, 'edge', scatter_dimension=0, tiled=True)  76.5 us
    reduce_scatter x1, waiting for transfers between devices, body(): lax.psum_scatter(sum_recv, 'edge', scatter_dimension=0, tiled=True)  76.3 us
    reduce_scatter x1, waiting for transfers between devices, body(): lax.psum_scatter(sum_edge, 'edge', scatter_dimension=0, tiled=True)  76 us
    reduce_scatter x1, waiting for transfers between devices, body(): lax.psum_scatter(sum_send, 'edge', scatter_dimension=0, tiled=True)  73.1 us
    dot_general x63, matrix products, transposed_times(): lax.dot_general(left, right, (((0,), (0,)), ((), ())), preferred_element_...  70.9 us
  transfers between devices with their start and end apart: 31, of which 22 were waited for; matrix products, arithmetic and copies ran while one was open for 5% of the time, Pallas kernels for 0%

commit v1 on v0

--- a/solution.py
+++ b/solution.py
@@ -149,7 +149,8 @@
         partial_back = to_nodes(send_grad, send_blocks, send_tiles) + to_nodes(
             recv_grad, recv_blocks, recv_tiles
         )
-        edge_terms = lax.psum(partial_back, "edge")
+        parts = lax.all_gather(partial_back, "edge", axis=0, tiled=False)
+        edge_terms = parts.sum(axis=0)
         node_out = (grad_nodes.astype(jnp.float32) + node_term + edge_terms).astype(jnp.bfloat16)
         fresh = (
             transposed_times(send_feats, edge_delta),

time: 2040 us -> 1950 us (0.956)
  waiting for transfers between devices: 946 us -> 782 us
  matrix products: 214 us -> 297 us
  local copies, waits for them, and re-layouts: 123 us -> 47.5 us
  other arithmetic: 2.35 us -> 64.2 us
    psum x9 -> x0, waiting for transfers between devices: 630 us -> none  [advance(): edge_terms = lax.psum(partial_back, 'edge')]
    all_gather x0 -> x9, waiting for transfers between devices: none -> 479 us  [advance(): parts = lax.all_gather(partial_back, 'edge', axis=0, tiled=False)]
    while x558 -> x414, local copies, waits for them, and re-layouts: 96.3 us -> 20.1 us
    dot_general x63, matrix products: 70.9 us -> 123 us  [transposed_times(): lax.dot_general(left, right, (((0,), (0,)), ((), ())), preferred_element_...]
    reduce_sum x0 -> x9, other arithmetic: none -> 39.6 us  [advance(): edge_terms = parts.sum(axis=0)]
    dot_general x54, matrix products: 16.2 us -> 45.2 us  [matmul(): return jnp.dot(left, right, preferred_element_type=jnp.float32)]
  transfers between devices with their start and end apart: 31 -> 31, of which waited for: 22 -> 13; matrix products, arithmetic and copies ran while one was open for 5% -> 10% of each run, Pallas kernels for 0% -> 0%
where the time goes in v1:
time: 1950 us; the launch traced here: 1940 us
  waiting for transfers between devices  782 us (40%)
  blocking collectives  707 us (36%)
  matrix products  297 us (15%)
  other arithmetic  64.2 us (3%)
  local copies, waits for them, and re-layouts  47.5 us (2%)
  starting transfers between devices  24.5 us (1%)
    psum x9, blocking collectives, advance(): aggregate = lax.psum(partial_agg, 'edge')  707 us
    all_gather x9, waiting for transfers between devices, advance(): parts = lax.all_gather(partial_back, 'edge', axis=0, tiled=False)  479 us
    dot_general x63, matrix products, transposed_times(): lax.dot_general(left, right, (((0,), (0,)), ((), ())), preferred_element_...  123 us
    reduce_scatter x1, waiting for transfers between devices, body(): lax.psum_scatter(sum_msg, 'edge', scatter_dimension=0, tiled=True)  76.5 us
    reduce_scatter x1, waiting for transfers between devices, body(): lax.psum_scatter(sum_recv, 'edge', scatter_dimension=0, tiled=True)  76.4 us
    reduce_scatter x1, waiting for transfers between devices, body(): lax.psum_scatter(sum_edge, 'edge', scatter_dimension=0, tiled=True)  76 us
    reduce_scatter x1, waiting for transfers between devices, body(): lax.psum_scatter(sum_send, 'edge', scatter_dimension=0, tiled=True)  71.8 us
    dot_general x63, matrix products, times_transposed(): lax.dot_general(left, right, (((1,), (1,)), ((), ())), preferred_element_...  49.7 us
  transfers between devices with their start and end apart: 31, of which 13 were waited for; matrix products, arithmetic and copies ran while one was open for 10% of the time, Pallas kernels for 0%

profile of v1, /device:TPU:0, one launch (start us, length us, event | category | flops | bytes accessed | tf_op | source)
XLA Modules:
  0.0 1941.8 jit_solution(3604530771544648667)
XLA Ops:
  13.5 1613.4 %while.36 = (s32[]{:T(128)}, bf16[256,512]{1,0:T(8,128)(2,1)}, bf16[256,512]{1,0:T(8,128)(2,1)S(1)}, f32[512,512]{1,0:T(8,128)}, f32[512,512]{1,0:T(8,128)}, /*i...) while((s32[]{:T(128)}, bf16[256,512]{1,0:T(8,128)(2,1)}, ...), condition=%wide.region_3.4_spmd.clone, body=%wide.region_0.3_spmd.clone.sunk | while | flops 2912428032 | bytes 141479168 | solution.py:187
  23.5 81.6 %all-reduce.1 = bf16[256,512]{1,0:T(8,128)(2,1)S(1)} all-reduce(f32[256,512]{1,0:T(8,128)S(1)} %bitcast.271), channel_id=1, replica_groups=mesh['section'=8,'edge'=16] {'edge'}, use_global_device_ids=true, to_apply=%region_1.1 | all-reduce | flops 131072 | bytes 786432 | tf_op jit(solution)/shard_map/while/body/eval_jaxpr/psum | solution.py:128
  127.3 57.1 %all-gather.2.cloned.1.call-done = f32[16,256,512]{2,1,0:T(8,128)} async-done(((f32[1,256,512]{2,1,0:T(8,128)}), f32[16,256,512]{2,1,0:T(8,128)}) %all-gather.2.cloned.1.call-update) | async-done | bytes 8388624 | tf_op jit(solution)/shard_map/while/body/eval_jaxpr/all_gather | solution.py:152
  184.5 4.4 reduce_sum.17
  204.8 78.2 %all-reduce.1 = bf16[256,512]{1,0:T(8,128)(2,1)S(1)} all-reduce(f32[256,512]{1,0:T(8,128)S(1)} %bitcast.271), channel_id=1, replica_groups=mesh['section'=8,'edge'=16] {'edge'}, use_global_device_ids=true, to_apply=%region_1.1 | all-reduce | flops 131072 | bytes 786432 | tf_op jit(solution)/shard_map/while/body/eval_jaxpr/psum | solution.py:128
  310.5 52.8 %all-gather.2.cloned.1.call-done = f32[16,256,512]{2,1,0:T(8,128)} async-done(((f32[1,256,512]{2,1,0:T(8,128)}), f32[16,256,512]{2,1,0:T(8,128)}) %all-gather.2.cloned.1.call-update) | async-done | bytes 8388624 | tf_op jit(solution)/shard_map/while/body/eval_jaxpr/all_gather | solution.py:152
  384.0 78.2 %all-reduce.1 = bf16[256,512]{1,0:T(8,128)(2,1)S(1)} all-reduce(f32[256,512]{1,0:T(8,128)S(1)} %bitcast.271), channel_id=1, replica_groups=mesh['section'=8,'edge'=16] {'edge'}, use_global_device_ids=true, to_apply=%region_1.1 | all-reduce | flops 131072 | bytes 786432 | tf_op jit(solution)/shard_map/while/body/eval_jaxpr/psum | solution.py:128
  489.6 52.7 %all-gather.2.cloned.1.call-done = f32[16,256,512]{2,1,0:T(8,128)} async-done(((f32[1,256,512]{2,1,0:T(8,128)}), f32[16,256,512]{2,1,0:T(8,128)}) %all-gather.2.cloned.1.call-update) | async-done | bytes 8388624 | tf_op jit(solution)/shard_map/while/body/eval_jaxpr/all_gather | solution.py:152
  563.0 78.1 %all-reduce.1 = bf16[256,512]{1,0:T(8,128)(2,1)S(1)} all-reduce(f32[256,512]{1,0:T(8,128)S(1)} %bitcast.271), channel_id=1, replica_groups=mesh['section'=8,'edge'=16] {'edge'}, use_global_device_ids=true, to_apply=%region_1.1 | all-reduce | flops 131072 | bytes 786432 | tf_op jit(solution)/shard_map/while/body/eval_jaxpr/psum | solution.py:128
  668.6 52.7 %all-gather.2.cloned.1.call-done = f32[16,256,512]{2,1,0:T(8,128)} async-done(((f32[1,256,512]{2,1,0:T(8,128)}), f32[16,256,512]{2,1,0:T(8,128)}) %all-gather.2.cloned.1.call-update) | async-done | bytes 8388624 | tf_op jit(solution)/shard_map/while/body/eval_jaxpr/all_gather | solution.py:152
  742.0 78.1 %all-reduce.1 = bf16[256,512]{1,0:T(8,128)(2,1)S(1)} all-reduce(f32[256,512]{1,0:T(8,128)S(1)} %bitcast.271), channel_id=1, replica_groups=mesh['section'=8,'edge'=16] {'edge'}, use_global_device_ids=true, to_apply=%region_1.1 | all-reduce | flops 131072 | bytes 786432 | tf_op jit(solution)/shard_map/while/body/eval_jaxpr/psum | solution.py:128
  847.6 52.7 %all-gather.2.cloned.1.call-done = f32[16,256,512]{2,1,0:T(8,128)} async-done(((f32[1,256,512]{2,1,0:T(8,128)}), f32[16,256,512]{2,1,0:T(8,128)}) %all-gather.2.cloned.1.call-update) | async-done | bytes 8388624 | tf_op jit(solution)/shard_map/while/body/eval_jaxpr/all_gather | solution.py:152
  921.0 78.2 %all-reduce.1 = bf16[256,512]{1,0:T(8,128)(2,1)S(1)} all-reduce(f32[256,512]{1,0:T(8,128)S(1)} %bitcast.271), channel_id=1, replica_groups=mesh['section'=8,'edge'=16] {'edge'}, use_global_device_ids=true, to_apply=%region_1.1 | all-reduce | flops 131072 | bytes 786432 | tf_op jit(solution)/shard_map/while/body/eval_jaxpr/psum | solution.py:128
  1026.6 52.7 %all-gather.2.cloned.1.call-done = f32[16,256,512]{2,1,0:T(8,128)} async-done(((f32[1,256,512]{2,1,0:T(8,128)}), f32[16,256,512]{2,1,0:T(8,128)}) %all-gather.2.cloned.1.call-update) | async-done | bytes 8388624 | tf_op jit(solution)/shard_map/while/body/eval_jaxpr/all_gather | solution.py:152
  1100.0 78.1 %all-reduce.1 = bf16[256,512]{1,0:T(8,128)(2,1)S(1)} all-reduce(f32[256,512]{1,0:T(8,128)S(1)} %bitcast.271), channel_id=1, replica_groups=mesh['section'=8,'edge'=16] {'edge'}, use_global_device_ids=true, to_apply=%region_1.1 | all-reduce | flops 131072 | bytes 786432 | tf_op jit(solution)/shard_map/while/body/eval_jaxpr/psum | solution.py:128
  1205.5 52.7 %all-gather.2.cloned.1.call-done = f32[16,256,512]{2,1,0:T(8,128)} async-done(((f32[1,256,512]{2,1,0:T(8,128)}), f32[16,256,512]{2,1,0:T(8,128)}) %all-gather.2.cloned.1.call-update) | async-done | bytes 8388624 | tf_op jit(solution)/shard_map/while/body/eval_jaxpr/all_gather | solution.py:152
  1278.9 78.1 %all-reduce.1 = bf16[256,512]{1,0:T(8,128)(2,1)S(1)} all-reduce(f32[256,512]{1,0:T(8,128)S(1)} %bitcast.271), channel_id=1, replica_groups=mesh['section'=8,'edge'=16] {'edge'}, use_global_device_ids=true, to_apply=%region_1.1 | all-reduce | flops 131072 | bytes 786432 | tf_op jit(solution)/shard_map/while/body/eval_jaxpr/psum | solution.py:128
  1384.5 52.7 %all-gather.2.cloned.1.call-done = f32[16,256,512]{2,1,0:T(8,128)} async-done(((f32[1,256,512]{2,1,0:T(8,128)}), f32[16,256,512]{2,1,0:T(8,128)}) %all-gather.2.cloned.1.call-update) | async-done | bytes 8388624 | tf_op jit(solution)/shard_map/while/body/eval_jaxpr/all_gather | solution.py:152
  1457.9 78.2 %all-reduce.1 = bf16[256,512]{1,0:T(8,128)(2,1)S(1)} all-reduce(f32[256,512]{1,0:T(8,128)S(1)} %bitcast.271), channel_id=1, replica_groups=mesh['section'=8,'edge'=16] {'edge'}, use_global_device_ids=true, to_apply=%region_1.1 | all-reduce | flops 131072 | bytes 786432 | tf_op jit(solution)/shard_map/while/body/eval_jaxpr/psum | solution.py:128
  1563.5 52.7 %all-gather.2.cloned.1.call-done = f32[16,256,512]{2,1,0:T(8,128)} async-done(((f32[1,256,512]{2,1,0:T(8,128)}), f32[16,256,512]{2,1,0:T(8,128)}) %all-gather.2.cloned.1.call-update) | async-done | bytes 8388624 | tf_op jit(solution)/shard_map/while/body/eval_jaxpr/all_gather | solution.py:152
  1633.8 71.8 %reduce-scatter.5.cloned.1.call-done = f32[32,512]{1,0:T(8,128)} async-done(((f32[512,512]{1,0:T(8,128)}), f32[32,512]{1,0:T(8,128)}) %reduce-scatter.5.cloned.1.call-update) | async-done | bytes 65552 | tf_op jit(solution)/shard_map/reduce_scatter | solution.py:191
  1705.7 76.4 %reduce-scatter.7.cloned.1.call-done = f32[32,512]{1,0:T(8,128)} async-done(((f32[512,512]{1,0:T(8,128)}), f32[32,512]{1,0:T(8,128)}) %reduce-scatter.7.cloned.1.call-update) | async-done | bytes 65552 | tf_op jit(solution)/shard_map/reduce_scatter | solution.py:192
  1782.0 76.0 %reduce-scatter.9.cloned.1.call-done = f32[32,512]{1,0:T(8,128)} async-done(((f32[512,512]{1,0:T(8,128)}), f32[32,512]{1,0:T(8,128)}) %reduce-scatter.9.cloned.1.call-update) | async-done | bytes 65552 | tf_op jit(solution)/shard_map/reduce_scatter | solution.py:193
  1858.0 76.5 %reduce-scatter.11.cloned.1.call-done = f32[32,512]{1,0:T(8,128)} async-done(((f32[512,512]{1,0:T(8,128)}), f32[32,512]{1,0:T(8,128)}) %reduce-scatter.11.cloned.1.call-update) | async-done | bytes 65552 | tf_op jit(solution)/shard_map/reduce_scatter | solution.py:194
  (854 shorter events, 430.9 us)
Async XLA Ops:
  13.5 170.9 %all-gather.2.cloned.1.call-start = ((), (), s32[]{:S(2)}) async-start(), calls=%async_computation.8 | async-start | bytes 8912896 | tf_op jit(solution)/shard_map/while/body/eval_jaxpr/all_gather | solution.py:152
  118.3 75.8 %collective-permute-start.1 = (bf16[256,512]{1,0:T(8,128)(2,1)}, bf16[256,512]{1,0:T(8,128)(2,1)S(1)}, u32[]{:S(2)}, u32[]{:S(2)}) collective-permute-start(bf16[256,512]{1,0:T(8,128)(2,1)} %get-tuple-element.1012), channel_id=1, source_target_pairs={{16,0},{32,16},{48,32},{64,48},{80,64},{96,80},{112,96},{17,1},{33... | collective-permute-start | bytes 786440 | tf_op jit(solution)/shard_map/while/body/eval_jaxpr/ppermute | solution.py:12
  194.8 168.5 %all-gather.2.cloned.1.call-start = ((), (), s32[]{:S(2)}) async-start(), calls=%async_computation.8 | async-start | bytes 8912896 | tf_op jit(solution)/shard_map/while/body/eval_jaxpr/all_gather | solution.py:152
  296.2 77.1 %collective-permute-start.1 = (bf16[256,512]{1,0:T(8,128)(2,1)}, bf16[256,512]{1,0:T(8,128)(2,1)S(1)}, u32[]{:S(2)}, u32[]{:S(2)}) collective-permute-start(bf16[256,512]{1,0:T(8,128)(2,1)} %get-tuple-element.1012), channel_id=1, source_target_pairs={{16,0},{32,16},{48,32},{64,48},{80,64},{96,80},{112,96},{17,1},{33... | collective-permute-start | bytes 786440 | tf_op jit(solution)/shard_map/while/body/eval_jaxpr/ppermute | solution.py:12
  368.1 5.3 collective-permute-start
  374.0 168.3 %all-gather.2.cloned.1.call-start = ((), (), s32[]{:S(2)}) async-start(), calls=%async_computation.8 | async-start | bytes 8912896 | tf_op jit(solution)/shard_map/while/body/eval_jaxpr/all_gather | solution.py:152
  475.4 77.0 %collective-permute-start.1 = (bf16[256,512]{1,0:T(8,128)(2,1)}, bf16[256,512]{1,0:T(8,128)(2,1)S(1)}, u32[]{:S(2)}, u32[]{:S(2)}) collective-permute-start(bf16[256,512]{1,0:T(8,128)(2,1)} %get-tuple-element.1012), channel_id=1, source_target_pairs={{16,0},{32,16},{48,32},{64,48},{80,64},{96,80},{112,96},{17,1},{33... | collective-permute-start | bytes 786440 | tf_op jit(solution)/shard_map/while/body/eval_jaxpr/ppermute | solution.py:12
  547.1 5.3 collective-permute-start
  553.0 168.3 %all-gather.2.cloned.1.call-start = ((), (), s32[]{:S(2)}) async-start(), calls=%async_computation.8 | async-start | bytes 8912896 | tf_op jit(solution)/shard_map/while/body/eval_jaxpr/all_gather | solution.py:152
  654.4 76.9 %collective-permute-start.1 = (bf16[256,512]{1,0:T(8,128)(2,1)}, bf16[256,512]{1,0:T(8,128)(2,1)S(1)}, u32[]{:S(2)}, u32[]{:S(2)}) collective-permute-start(bf16[256,512]{1,0:T(8,128)(2,1)} %get-tuple-element.1012), channel_id=1, source_target_pairs={{16,0},{32,16},{48,32},{64,48},{80,64},{96,80},{112,96},{17,1},{33... | collective-permute-start | bytes 786440 | tf_op jit(solution)/shard_map/while/body/eval_jaxpr/ppermute | solution.py:12
  732.0 168.3 %all-gather.2.cloned.1.call-start = ((), (), s32[]{:S(2)}) async-start(), calls=%async_computation.8 | async-start | bytes 8912896 | tf_op jit(solution)/shard_map/while/body/eval_jaxpr/all_gather | solution.py:152
  833.3 77.0 %collective-permute-start.1 = (bf16[256,512]{1,0:T(8,128)(2,1)}, bf16[256,512]{1,0:T(8,128)(2,1)S(1)}, u32[]{:S(2)}, u32[]{:S(2)}) collective-permute-start(bf16[256,512]{1,0:T(8,128)(2,1)} %get-tuple-element.1012), channel_id=1, source_target_pairs={{16,0},{32,16},{48,32},{64,48},{80,64},{96,80},{112,96},{17,1},{33... | collective-permute-start | bytes 786440 | tf_op jit(solution)/shard_map/while/body/eval_jaxpr/ppermute | solution.py:12
  911.0 168.3 %all-gather.2.cloned.1.call-start = ((), (), s32[]{:S(2)}) async-start(), calls=%async_computation.8 | async-start | bytes 8912896 | tf_op jit(solution)/shard_map/while/body/eval_jaxpr/all_gather | solution.py:152
  1012.3 76.9 %collective-permute-start.1 = (bf16[256,512]{1,0:T(8,128)(2,1)}, bf16[256,512]{1,0:T(8,128)(2,1)S(1)}, u32[]{:S(2)}, u32[]{:S(2)}) collective-permute-start(bf16[256,512]{1,0:T(8,128)(2,1)} %get-tuple-element.1012), channel_id=1, source_target_pairs={{16,0},{32,16},{48,32},{64,48},{80,64},{96,80},{112,96},{17,1},{33... | collective-permute-start | bytes 786440 | tf_op jit(solution)/shard_map/while/body/eval_jaxpr/ppermute | solution.py:12
  1090.0 168.3 %all-gather.2.cloned.1.call-start = ((), (), s32[]{:S(2)}) async-start(), calls=%async_computation.8 | async-start | bytes 8912896 | tf_op jit(solution)/shard_map/while/body/eval_jaxpr/all_gather | solution.py:152
  1191.3 76.9 %collective-permute-start.1 = (bf16[256,512]{1,0:T(8,128)(2,1)}, bf16[256,512]{1,0:T(8,128)(2,1)S(1)}, u32[]{:S(2)}, u32[]{:S(2)}) collective-permute-start(bf16[256,512]{1,0:T(8,128)(2,1)} %get-tuple-element.1012), channel_id=1, source_target_pairs={{16,0},{32,16},{48,32},{64,48},{80,64},{96,80},{112,96},{17,1},{33... | collective-permute-start | bytes 786440 | tf_op jit(solution)/shard_map/while/body/eval_jaxpr/ppermute | solution.py:12
  1268.9 168.3 %all-gather.2.cloned.1.call-start = ((), (), s32[]{:S(2)}) async-start(), calls=%async_computation.8 | async-start | bytes 8912896 | tf_op jit(solution)/shard_map/while/body/eval_jaxpr/all_gather | solution.py:152
  1370.3 77.0 %collective-permute-start.1 = (bf16[256,512]{1,0:T(8,128)(2,1)}, bf16[256,512]{1,0:T(8,128)(2,1)S(1)}, u32[]{:S(2)}, u32[]{:S(2)}) collective-permute-start(bf16[256,512]{1,0:T(8,128)(2,1)} %get-tuple-element.1012), channel_id=1, source_target_pairs={{16,0},{32,16},{48,32},{64,48},{80,64},{96,80},{112,96},{17,1},{33... | collective-permute-start | bytes 786440 | tf_op jit(solution)/shard_map/while/body/eval_jaxpr/ppermute | solution.py:12
  1447.9 168.3 %all-gather.2.cloned.1.call-start = ((), (), s32[]{:S(2)}) async-start(), calls=%async_computation.8 | async-start | bytes 8912896 | tf_op jit(solution)/shard_map/while/body/eval_jaxpr/all_gather | solution.py:152
  1549.3 76.9 %collective-permute-start.1 = (bf16[256,512]{1,0:T(8,128)(2,1)}, bf16[256,512]{1,0:T(8,128)(2,1)S(1)}, u32[]{:S(2)}, u32[]{:S(2)}) collective-permute-start(bf16[256,512]{1,0:T(8,128)(2,1)} %get-tuple-element.1012), channel_id=1, source_target_pairs={{16,0},{32,16},{48,32},{64,48},{80,64},{96,80},{112,96},{17,1},{33... | collective-permute-start | bytes 786440 | tf_op jit(solution)/shard_map/while/body/eval_jaxpr/ppermute | solution.py:12
  1626.9 78.7 %reduce-scatter.5.cloned.1.call-start = ((), (), s32[]{:S(2)}) async-start(), calls=%async_computation.4 | async-start | bytes 1114112 | tf_op jit(solution)/shard_map/reduce_scatter | solution.py:191
  1627.5 154.5 %reduce-scatter.7.cloned.1.call-start = ((), (), s32[]{:S(2)}) async-start(), calls=%async_computation.5 | async-start | bytes 1114112 | tf_op jit(solution)/shard_map/reduce_scatter | solution.py:192
  1628.1 229.9 %reduce-scatter.9.cloned.1.call-start = ((), (), s32[]{:S(2)}) async-start(), calls=%async_computation.6 | async-start | bytes 1114112 | tf_op jit(solution)/shard_map/reduce_scatter | solution.py:193
  1628.7 305.8 %reduce-scatter.11.cloned.1.call-start = ((), (), s32[]{:S(2)}) async-start(), calls=%async_computation.7 | async-start | bytes 1114112 | tf_op jit(solution)/shard_map/reduce_scatter | solution.py:194
  (214 other events, 4384.9 us)
Sparse Core Ops, SparseCore 0:
  116.2 68.2 all-gather.1
  294.2 69.0 all-gather.1
  473.3 68.9 all-gather.1
  652.3 68.9 all-gather.1
  831.3 68.9 all-gather.1
  1010.3 68.9 all-gather.1
  1189.2 68.9 all-gather.1
  1368.2 68.9 all-gather.1
  1547.2 68.9 all-gather.1
Sparse Core Ops, SparseCore 1:
  1631.2 74.4 reduce-scatter.4
  1709.6 72.3 reduce-scatter.6
  1785.7 72.3 reduce-scatter.8
  1862.1 72.3 reduce-scatter.10
